TPU v7x, 32 devices: a whole 2x2x4 slice. The times are simulated.
32 devices in a mesh: groups: 2 (over x), row: 16 (over z, y, core).
Axes of the slice: x: 2, y: 2, z: 4, core: 2. Of those that a mesh axis runs over, the one named last changes fastest.
Arguments:
- features: bfloat16 [128, 64, 512], P(('groups', 'row')), parts along dimension 0, may hold values from -6 to 6
- cotangent: bfloat16 [128, 64, 512], P(('groups', 'row')), parts along dimension 0, may hold values from -6 to 6
- depth_weight: bfloat16 [49, 512], P(None, 'row'), may hold values from -0.875 to 0.875
- depth_bias: bfloat16 [512], P('row'), may hold values from -3 to 3
- norm_gain: bfloat16 [512], P('row'), may hold values from 0.25 to 1.75
- norm_shift: bfloat16 [512], P('row'), may hold values from -3 to 3
- up_weight: bfloat16 [512, 2048], P('row'), may hold values from -0.25 to 0.25
- up_bias: bfloat16 [2048], P('row'), may hold values from -3 to 3
- down_weight: bfloat16 [2048, 512], P('row'), may hold values from -0.125 to 0.125
- down_bias: bfloat16 [512], P('row'), may hold values from -3 to 3
Outputs:
- block_out: bfloat16 [128, 64, 512], P(('groups', 'row')), parts along dimension 0
- grad_features: bfloat16 [128, 64, 512], P(('groups', 'row')), parts along dimension 0
- grad_up_weight: float32 [1024, 2048], P(('groups', 'row')), parts along dimension 0
- grad_down_weight: float32 [4096, 512], P(('groups', 'row')), parts along dimension 0
- grad_depth_weight: float32 [98, 512], P('groups', 'row'), parts along dimension 0
- grad_depth_bias: float32 [1024], P(('groups', 'row')), parts along dimension 0
- grad_norm_gain: float32 [1024], P(('groups', 'row')), parts along dimension 0
- grad_norm_shift: float32 [1024], P(('groups', 'row')), parts along dimension 0
- grad_up_bias: float32 [4096], P(('groups', 'row')), parts along dimension 0
- grad_down_bias: float32 [1024], P(('groups', 'row')), parts along dimension 0
There are 2 independent parts, one for each index of `groups`. A program takes and returns all parts, laid end to end along the dimension named above; an argument that names none is the same for every part. Nothing has to cross between parts.
All inputs are finite; a program needn't handle non-finite values.
Results may differ from a plain program's by a relative error of at most 0.0055.
Values may be sent and summed in bfloat16 or wider, within the bound.
A program may use at most 64 MiB of HBM per device.

v0:
```python
import math
import jax
import jax.numpy as jnp
from jax import lax
from jax.sharding import PartitionSpec as P

eps = 1e-06


def with_halo(block, sides, width):
    for axis, dim in sides:
        count = lax.axis_size(axis)
        forward = [(i, i + 1) for i in range(count - 1)]
        backward = [(target, source) for source, target in forward]
        low = lax.ppermute(
            lax.slice_in_dim(block, block.shape[dim] - width, None, axis=dim), axis, forward
        )
        high = lax.ppermute(lax.slice_in_dim(block, 0, width, axis=dim), axis, backward)
        block = jnp.concatenate([low, block, high], axis=dim)
    return block


def gelu_value(value):
    return 0.5 * value * (1.0 + lax.erf(value * (1.0 / math.sqrt(2.0))))


def gelu_slope(value):
    cumulative = 0.5 * (1.0 + lax.erf(value * (1.0 / math.sqrt(2.0))))
    density = jnp.exp(-0.5 * value * value) * (1.0 / math.sqrt(2.0 * math.pi))
    return cumulative + value * density


def depth_conv(padded, kernel, height, width):
    total = jnp.zeros((height, width, kernel.shape[1]), jnp.float32)
    for first in range(7):
        for second in range(7):
            total = (
                total
                + padded[first : first + height, second : second + width, :]
                * kernel[first * 7 + second]
            )
    return total


def depth_conv_back(padded, kernel, height, width):
    total = jnp.zeros((height, width, kernel.shape[1]), jnp.float32)
    for first in range(7):
        for second in range(7):
            total = (
                total
                + padded[6 - first : 6 - first + height, 6 - second : 6 - second + width, :]
                * kernel[first * 7 + second]
            )
    return total


def per_device(
    features,
    cotangent,
    depth_weight,
    depth_bias,
    norm_gain,
    norm_shift,
    up_weight,
    up_bias,
    down_weight,
    down_bias,
):
    height, width, chans = features.shape
    devices = lax.axis_size("row")
    cells = height * width
    scale = 1.0 / math.sqrt(cells * devices)
    kernel, conv_bias, gain, shift, bias_down, bias_up = (
        lax.all_gather(depth_weight, "row", axis=1, tiled=True),
        lax.all_gather(depth_bias, "row", axis=0, tiled=True),
        lax.all_gather(norm_gain, "row", axis=0, tiled=True),
        lax.all_gather(norm_shift, "row", axis=0, tiled=True),
        lax.all_gather(down_bias, "row", axis=0, tiled=True),
        lax.all_gather(up_bias, "row", axis=0, tiled=True),
    )
    kernel = kernel.astype(jnp.float32)
    gain = gain.astype(jnp.float32)
    rimmed = with_halo(features, (("row", 0),), 3)
    padded = jnp.pad(rimmed.astype(jnp.float32), ((0, 0), (3, 3), (0, 0)))
    conv = depth_conv(padded, kernel, height, width) + conv_bias.astype(jnp.float32)
    mean_val = jnp.mean(conv, axis=2, keepdims=True)
    centered = conv - mean_val
    var_val = jnp.mean(centered * centered, axis=2, keepdims=True)
    inv = lax.rsqrt(var_val + eps)
    normed = centered * inv
    normal_out = (normed * gain + shift.astype(jnp.float32)).astype(jnp.bfloat16)
    flat_norm = normal_out.reshape(cells, chans)
    flat_cot = cotangent.reshape(cells, chans)
    columns = flat_norm
    hidden = jnp.dot(
        columns,
        lax.all_gather(up_weight, "row", axis=0, tiled=True),
        preferred_element_type=jnp.float32,
    ) + bias_up.astype(jnp.float32)
    act = gelu_value(hidden).astype(jnp.bfloat16)
    columns = act
    mixed = jnp.dot(
        columns,
        lax.all_gather(down_weight, "row", axis=0, tiled=True),
        preferred_element_type=jnp.float32,
    )
    block_out = (
        features.astype(jnp.float32)
        + (mixed + bias_down.astype(jnp.float32)).reshape(height, width, chans)
    ).astype(jnp.bfloat16)
    down_full = (
        lax.dot_general(act, flat_cot, (((0,), (0,)), ((), ())), preferred_element_type=jnp.float32)
        * scale
    )
    grad_down_weight = lax.psum_scatter(down_full, "row", scatter_dimension=0, tiled=True)
    dact = lax.dot_general(
        flat_cot,
        lax.all_gather(down_weight, "row", axis=0, tiled=True),
        (((1,), (1,)), ((), ())),
        preferred_element_type=jnp.float32,
    )
    dhidden = (dact * gelu_slope(hidden)).astype(jnp.bfloat16)
    columns = flat_norm
    grad_up_weight = lax.psum_scatter(
        lax.dot_general(
            columns, dhidden, (((0,), (0,)), ((), ())), preferred_element_type=jnp.float32
        )
        * scale,
        "row",
        scatter_dimension=0,
        tiled=True,
    )
    dnorm = lax.dot_general(
        dhidden,
        lax.all_gather(up_weight, "row", axis=0, tiled=True),
        (((1,), (1,)), ((), ())),
        preferred_element_type=jnp.float32,
    )
    dnorm = dnorm.reshape(height, width, chans)
    down_bias_term = jnp.sum(flat_cot.astype(jnp.float32), axis=0) * scale
    up_bias_term = jnp.sum(dhidden.astype(jnp.float32), axis=0) * scale
    gain_term = jnp.sum(dnorm * normed, axis=(0, 1)) * scale
    shift_term = jnp.sum(dnorm, axis=(0, 1)) * scale
    grad_down_bias, grad_up_bias, grad_norm_gain, grad_norm_shift = (
        lax.psum_scatter(down_bias_term, "row", scatter_dimension=0, tiled=True),
        lax.psum_scatter(up_bias_term, "row", scatter_dimension=0, tiled=True),
        lax.psum_scatter(gain_term, "row", scatter_dimension=0, tiled=True),
        lax.psum_scatter(shift_term, "row", scatter_dimension=0, tiled=True),
    )
    scaled = dnorm * gain
    dconv = inv * (
        scaled
        - jnp.mean(scaled, axis=2, keepdims=True)
        - normed * jnp.mean(scaled * normed, axis=2, keepdims=True)
    )
    dconv = dconv.astype(jnp.bfloat16)
    dconv_wide = dconv.astype(jnp.float32)
    back_rim = with_halo(dconv, (("row", 0),), 3)
    back_pad = jnp.pad(back_rim.astype(jnp.float32), ((0, 0), (3, 3), (0, 0)))
    grad_features = (
        cotangent.astype(jnp.float32) + depth_conv_back(back_pad, kernel, height, width)
    ).astype(jnp.bfloat16)
    taps = []
    for first in range(7):
        for second in range(7):
            taps.append(
                jnp.sum(
                    dconv_wide * padded[first : first + height, second : second + width, :],
                    axis=(0, 1),
                )
            )
    kernel_term = jnp.stack(taps, axis=0) * scale
    conv_bias_term = jnp.sum(dconv_wide, axis=(0, 1)) * scale
    grad_depth_weight, grad_depth_bias = (
        lax.psum_scatter(kernel_term, "row", scatter_dimension=1, tiled=True),
        lax.psum_scatter(conv_bias_term, "row", scatter_dimension=0, tiled=True),
    )
    return (
        block_out,
        grad_features,
        grad_up_weight,
        grad_down_weight,
        grad_depth_weight,
        grad_depth_bias,
        grad_norm_gain,
        grad_norm_shift,
        grad_up_bias,
        grad_down_bias,
    )


def solution(mesh):
    placed = (
        P(("groups", "row"), None, None),
        P(("groups", "row"), None, None),
        P(None, "row"),
        P("row"),
        P("row"),
        P("row"),
        P("row", None),
        P("row"),
        P("row", None),
        P("row"),
    )
    return jax.shard_map(
        per_device,
        mesh=mesh,
        in_specs=placed,
        out_specs=(
            P(("groups", "row"), None, None),
            P(("groups", "row"), None, None),
            P(("groups", "row"), None),
            P(("groups", "row"), None),
            P("groups", "row"),
            P(("groups", "row")),
            P(("groups", "row")),
            P(("groups", "row")),
            P(("groups", "row")),
            P(("groups", "row")),
        ),
        check_vma=False,
    )
```

profile of v0, /device:TPU:0, one launch (start us, length us, event | category | flops | bytes accessed | tf_op | source)
XLA Modules:
  0.0 336.8 jit_solution(5923359344454385601)
XLA Ops:
  7.2 0.0 all-gather.4.cloned.1.call-start
  7.2 0.7 all-gather.4.cloned.1.call-update
  7.9 0.0 all-gather.6.cloned.1.call-start
  8.0 0.7 all-gather.6.cloned.1.call-update
  8.7 0.0 reduce-scatter.10.cloned.1.call-start
  8.7 1.1 fusion.148
  9.8 2.4 collective-permute-start
  12.2 1.3 collective-permute-start.1
  13.5 25.6 %all_gather.26 = bf16[49,512]{0,1:T(8,128)(2,1)S(1)} all-gather(bf16[49,32]{0,1:T(8,128)(2,1)} %param.12), channel_id=1, replica_groups=mesh['groups'=2,'row'=16] {'row'}, dimensions={1}, use_global_device_ids=true | all-gather | bytes 53312 | tf_op jit(solution)/shard_map/all_gather | solution.py:74
  39.1 2.6 slice_reduce_fusion.48
  41.8 0.0 copy-start.62
  41.8 0.0 copy-start.66
  41.8 0.0 copy-start.67
  41.8 1.6 slice_reduce_fusion.46
  43.5 0.6 fusion.149
  44.7 0.2 dynamic-update-slice
  45.0 0.2 dynamic-update-slice.1
  45.2 0.2 dynamic-update-slice.2
  45.5 0.2 dynamic-update-slice.3
  45.7 30.5 %all-reduce.12 = (bf16[512]{0:T(512)(128)(2,1)S(1)}, bf16[512]{0:T(512)(128)(2,1)S(1)}, bf16[512]{0:T(512)(128)(2,1)S(1)}, bf16[512]{0:T(512)(128)(2,1)}) all-reduce(bf16[512]{0:T(512)(128)(2,1)S(1)} %dynamic-update-slice, bf16[512]{0:T(512)(128)(2,1)S(1)} %dynamic-update-slice.2, ...), channel_id=1, replica_groups=mesh['groups'=2,'row'=16] {'row'}, use_global_device_ids=true, to_apply=%add.2 | all-reduce | flops 2048 | bytes 8192
  76.2 17.5 %all-gather = bf16[16,1,128]{2,1,0:T(2,128)(2,1)S(1)} all-gather(bf16[1,1,128]{2,1,0:T(2,128)(2,1)S(1)} %bitcast.131), channel_id=1, replica_groups=mesh['groups'=2,'row'=16] {'row'}, dimensions={0}, use_global_device_ids=true | all-gather | bytes 4352 | tf_op jit(solution)/shard_map/all_gather | solution.py:79
  93.8 2.7 slice_reduce_fusion.47
  96.7 0.1 maximum_convert_fusion
  96.8 4.7 %fusion.146 = (f32[4,64]{1,0:T(4,128)S(1)}, f32[4,64,512]{2,1,0:T(8,128)S(1)}) fusion(f32[512]{0:T(512)S(1)} %convert_element_type.62, f32[512]{0:T(512)S(1)} %get-tuple-element.85, f32[512]{0:T(512)S(1)} %get-tuple-element.86, f32[512]{0:T(512)S(1)} %get-tuple-element.87, f32[512]{0:T(512)S(1)} %get-tuple-element.88, ...), kind=kLoop, calls=%fused_computation.368 | loop fusion | flops 12975872 | bytes 5608448 | tf_op jit(solution)/shard_map/reduce_sum | solution.py:86
  101.7 0.2 multiply_reduce_fusion.3
  101.9 0.2 add_convert_fusion.1
  102.1 0.0 copy-start.2
  102.1 0.0 all-gather.4.cloned.1.call-done
  102.1 3.8 %multiply_convert_fusion = (bf16[256,2048]{1,0:T(8,128)(2,1)S(1)}, f32[256,2048]{1,0:T(8,128)}) fusion(f32[2048]{0:T(1024)S(1)} %bitcast.81, bf16[256,512]{1,0:T(8,128)(2,1)S(1)} %bitcast.75, bf16[512,2048]{1,0:T(8,128)(2,1)} %all-gather.4.cloned.1.call-done), kind=kOutput, calls=%fused_computation.61 | convolution fusion | flops 540016640 | bytes 5513216 | tf_op jit(solution)/shard_map/dot_general | solution.py:95
  106.0 4.2 %convert_reduce_fusion.1 = (f32[2048]{0:T(1024)}, bf16[256,2048]{1,0:T(8,128)(2,1)S(1)}) fusion(f32[256,2048]{1,0:T(8,128)} %get-tuple-element.152, bf16[256,512]{1,0:T(8,128)(2,1)} %bitcast.77, bf16[2048,512]{1,0:T(8,128)(2,1)} %all-gather.6.cloned.1.call-done), kind=kOutput, calls=%fused_computation.60 | convolution fusion | flops 543160320 | bytes 5513216 | tf_op jit(solution)/shard_map/dot_general | solution.py:116
  110.2 1.3 fusion.145
  111.5 0.8 copy-done
  112.3 0.8 multiply_reduce_fusion
  113.1 0.6 broadcast_multiply_fusion.6
  113.7 0.7 div.17
  114.4 3.2 fusion.143
  117.5 1.4 fusion.142
  119.1 0.0 copy-start.3
  119.1 1.0 fusion.144
  120.3 2.3 stack.199
  122.6 0.9 copy.22
  123.5 0.0 reduce-scatter.10.cloned.1.call-update
  123.5 0.3 reduce-scatter.6.cloned.1.call-start
  123.8 3.9 %convolution_multiply_fusion.1 = f32[512,2048]{1,0:T(8,128)} fusion(bf16[256,512]{1,0:T(8,128)(2,1)S(1)} %bitcast.76, bf16[256,2048]{1,0:T(8,128)(2,1)} %copy-done.6), kind=kOutput, calls=%fused_computation.51 | convolution fusion | flops 537919488 | bytes 5505024 | tf_op jit(solution)/shard_map/dot_general | solution.py:125
  127.7 0.0 reduce-scatter.6.cloned.1.call-update
  127.7 0.0 reduce-scatter.8.cloned.1.call-start
  127.7 0.9 copy-done.4
  128.6 2.7 convolution_multiply_fusion
  131.3 0.0 reduce-scatter.8.cloned.1.call-update
  132.7 0.1 convert_reduce_fusion.2
  132.8 59.3 %all-reduce.11 = (f32[512]{0:T(512)S(1)}, f32[512]{0:T(512)S(1)}, f32[512]{0:T(512)S(1)}, f32[2048]{0:T(1024)S(1)}, f32[512]{0:T(512)S(1)}) all-reduce(f32[512]{0:T(512)S(1)} %broadcast_multiply_fusion.5, f32[512]{0:T(512)S(1)} %get-tuple-element.157, ...), channel_id=5, replica_groups=mesh['groups'=2,'row'=16] {'row'}, use_global_device_ids=true, to_apply=%region_57.58.clone | all-reduce | flops 4096 | bytes 32768
  192.1 0.6 dynamic-slice.13
  192.7 0.6 dynamic-slice.9
  193.3 0.6 dynamic-slice.7
  193.9 0.6 dynamic-slice.5
  194.5 1.3 collective-permute-start.2
  195.8 1.3 collective-permute-start.3
  197.1 0.6 dynamic-slice.11
  197.7 2.4 convolution_add_fusion.1
  200.3 0.8 add_convert_fusion
  201.1 0.1 maximum_convert_fusion.1
  201.4 4.7 %fusion.5 = bf16[4,64,512]{2,1,0:T(8,128)(2,1)} fusion(bf16[4,64,512]{2,1,0:T(8,128)(2,1)S(1)} %copy-done.4, f32[10,64,512]{2,1,0:T(8,128)S(1)} %maximum_convert_fusion.1, f32[512]{0:T(512)S(1)} %get-tuple-element.85, f32[512]{0:T(512)S(1)} %get-tuple-element.86, f32[512]{0:T(512)S(1)} %get-tuple-element.87, f32[512]{0:T(512)S(1)} %get-tuple-element.88, ...), kind=kLoop, calls=%fused_computation.152 | loop fusion | flops 13107200 | bytes 5605376 | tf_op jit(solution)/shard_map/convert_element_type | solution.py:162
  206.0 48.2 %reduce-scatter.6.cloned.1.call-done = f32[32,2048]{1,0:T(8,128)} async-done(((f32[512,2048]{1,0:T(8,128)}), f32[32,2048]{1,0:T(8,128)}) %reduce-scatter.6.cloned.1.call-update) | async-done | bytes 262160 | tf_op jit(solution)/shard_map/reduce_scatter | solution.py:124
  254.2 76.1 %reduce-scatter.8.cloned.1.call-done = f32[128,512]{1,0:T(8,128)} async-done(((f32[2048,512]{1,0:T(8,128)}), f32[128,512]{1,0:T(8,128)}) %reduce-scatter.8.cloned.1.call-update) | async-done | bytes 262160 | tf_op jit(solution)/shard_map/reduce_scatter | solution.py:115
  (158 shorter events, 0.4 us)
Async XLA Ops:
  7.2 94.9 %all-gather.4.cloned.1.call-start = ((), (), s32[]{:S(2)}) async-start(), calls=%async_computation.3 | async-start | bytes 2228224 | tf_op jit(solution)/shard_map/all_gather | solution.py:97
  7.9 98.0 %all-gather.6.cloned.1.call-start = ((), (), s32[]{:S(2)}) async-start(), calls=%async_computation.4 | async-start | bytes 2228224 | tf_op jit(solution)/shard_map/all_gather | solution.py:104
  8.7 197.4 %reduce-scatter.10.cloned.1.call-start = ((), (), s32[]{:S(2)}) async-start(), calls=%async_computation.7 | async-start | bytes 278528
  9.8 86.9 %collective-permute-start = (bf16[3,64,512]{2,1,0:T(8,128)(2,1)S(1)}, bf16[3,64,512]{2,1,0:T(8,128)(2,1)S(1)}, u32[]{:S(2)}, u32[]{:S(2)}) collective-permute-start(bf16[3,64,512]{2,1,0:T(8,128)(2,1)S(1)} %get-tuple-element.147), channel_id=1, source_target_pairs={{0,1},{1,2},{2,3},{3,4},{4,5},{5,6},{6,7},{7,8},{8,9},{9,10},{10,1... | collective-permute-start | bytes 589832 | tf_op jit(solution)/shard_map/ppermute | solution.py:15
  12.2 84.5 %collective-permute-start.1 = (bf16[3,64,512]{2,1,0:T(8,128)(2,1)S(1)}, bf16[3,64,512]{2,1,0:T(8,128)(2,1)S(1)}, u32[]{:S(2)}, u32[]{:S(2)}) collective-permute-start(bf16[3,64,512]{2,1,0:T(8,128)(2,1)S(1)} %get-tuple-element.148), channel_id=1, source_target_pairs={{1,0},{2,1},{3,2},{4,3},{5,4},{6,5},{7,6},{8,7},{9,8},{10,9},{11,1... | collective-permute-start | bytes 589832 | tf_op jit(solution)/shard_map/ppermute | solution.py:18
  41.8 1.7 copy-start.62
  41.8 2.9 copy-start.66
  41.8 3.2 copy-start.67
  41.8 3.4 %copy-start.68 = (bf16[32]{0:T(256)(128)(2,1)S(1)}, bf16[32]{0:T(256)(128)(2,1)}, u32[]{:S(2)}) copy-start(bf16[32]{0:T(256)(128)(2,1)} %param.15) | copy-start | bytes 196
  41.8 3.7 %copy-start.69 = (bf16[32]{0:T(256)(128)(2,1)S(1)}, bf16[32]{0:T(256)(128)(2,1)}, u32[]{:S(2)}) copy-start(bf16[32]{0:T(256)(128)(2,1)} %param.19) | copy-start | bytes 196
  41.8 34.4 %copy-start.65 = (bf16[128]{0:T(256)(128)(2,1)S(1)}, bf16[128]{0:T(256)(128)(2,1)}, u32[]{:S(2)}) copy-start(bf16[128]{0:T(256)(128)(2,1)} %param.17) | copy-start | bytes 772
  93.8 2.9 copy-start.1
  96.5 5.0 %copy-start.7 = (f32[512]{0:T(512)}, f32[512]{0:T(512)S(1)}, u32[]{:S(2)}) copy-start(f32[512]{0:T(512)S(1)} %get-tuple-element.104) | copy-start | bytes 6148
  96.5 5.0 %copy-start.9 = (f32[512]{0:T(512)}, f32[512]{0:T(512)S(1)}, u32[]{:S(2)}) copy-start(f32[512]{0:T(512)S(1)} %get-tuple-element.105) | copy-start | bytes 6148
  96.5 5.0 %copy-start.11 = (f32[512]{0:T(512)}, f32[512]{0:T(512)S(1)}, u32[]{:S(2)}) copy-start(f32[512]{0:T(512)S(1)} %get-tuple-element.106) | copy-start | bytes 6148
  96.5 5.0 %copy-start.13 = (f32[512]{0:T(512)}, f32[512]{0:T(512)S(1)}, u32[]{:S(2)}) copy-start(f32[512]{0:T(512)S(1)} %get-tuple-element.107) | copy-start | bytes 6148
  96.5 5.0 %copy-start.15 = (f32[512]{0:T(512)}, f32[512]{0:T(512)S(1)}, u32[]{:S(2)}) copy-start(f32[512]{0:T(512)S(1)} %get-tuple-element.108) | copy-start | bytes 6148
  96.5 5.0 %copy-start.17 = (f32[512]{0:T(512)}, f32[512]{0:T(512)S(1)}, u32[]{:S(2)}) copy-start(f32[512]{0:T(512)S(1)} %get-tuple-element.109) | copy-start | bytes 6148
  96.5 5.0 %copy-start.19 = (f32[512]{0:T(512)}, f32[512]{0:T(512)S(1)}, u32[]{:S(2)}) copy-start(f32[512]{0:T(512)S(1)} %get-tuple-element.110) | copy-start | bytes 6148
  96.5 5.0 %copy-start.21 = (f32[512]{0:T(512)}, f32[512]{0:T(512)S(1)}, u32[]{:S(2)}) copy-start(f32[512]{0:T(512)S(1)} %get-tuple-element.111) | copy-start | bytes 6148
  96.6 5.0 %copy-start.23 = (f32[512]{0:T(512)}, f32[512]{0:T(512)S(1)}, u32[]{:S(2)}) copy-start(f32[512]{0:T(512)S(1)} %get-tuple-element.112) | copy-start | bytes 6148
  96.6 5.0 %copy-start.25 = (f32[512]{0:T(512)}, f32[512]{0:T(512)S(1)}, u32[]{:S(2)}) copy-start(f32[512]{0:T(512)S(1)} %get-tuple-element.113) | copy-start | bytes 6148
  96.6 5.0 %copy-start.27 = (f32[512]{0:T(512)}, f32[512]{0:T(512)S(1)}, u32[]{:S(2)}) copy-start(f32[512]{0:T(512)S(1)} %get-tuple-element.114) | copy-start | bytes 6148
  96.6 5.0 %copy-start.29 = (f32[512]{0:T(512)}, f32[512]{0:T(512)S(1)}, u32[]{:S(2)}) copy-start(f32[512]{0:T(512)S(1)} %get-tuple-element.115) | copy-start | bytes 6148
  96.6 5.0 %copy-start.31 = (f32[512]{0:T(512)}, f32[512]{0:T(512)S(1)}, u32[]{:S(2)}) copy-start(f32[512]{0:T(512)S(1)} %get-tuple-element.116) | copy-start | bytes 6148
  96.6 5.0 %copy-start.33 = (f32[512]{0:T(512)}, f32[512]{0:T(512)S(1)}, u32[]{:S(2)}) copy-start(f32[512]{0:T(512)S(1)} %get-tuple-element.117) | copy-start | bytes 6148
  96.6 5.0 %copy-start.35 = (f32[512]{0:T(512)}, f32[512]{0:T(512)S(1)}, u32[]{:S(2)}) copy-start(f32[512]{0:T(512)S(1)} %get-tuple-element.118) | copy-start | bytes 6148
  96.6 5.0 %copy-start.37 = (f32[512]{0:T(512)}, f32[512]{0:T(512)S(1)}, u32[]{:S(2)}) copy-start(f32[512]{0:T(512)S(1)} %get-tuple-element.119) | copy-start | bytes 6148
  96.6 5.0 %copy-start.39 = (f32[512]{0:T(512)}, f32[512]{0:T(512)S(1)}, u32[]{:S(2)}) copy-start(f32[512]{0:T(512)S(1)} %get-tuple-element.120) | copy-start | bytes 6148
  96.7 5.0 %copy-start.41 = (f32[512]{0:T(512)}, f32[512]{0:T(512)S(1)}, u32[]{:S(2)}) copy-start(f32[512]{0:T(512)S(1)} %get-tuple-element.121) | copy-start | bytes 6148
  102.1 3.9 %copy-start.2 = (bf16[4,64,512]{2,1,0:T(8,128)(2,1)}, bf16[4,64,512]{2,1,0:T(8,128)(2,1)S(1)}, u32[]{:S(2)}) copy-start(bf16[4,64,512]{2,1,0:T(8,128)(2,1)S(1)} %add_convert_fusion.1) | copy-start | bytes 786436
  106.0 4.2 %copy-start.5 = (bf16[512,2048]{1,0:T(8,128)(2,1)S(1)}, bf16[512,2048]{1,0:T(8,128)(2,1)}, u32[]{:S(2)}) copy-start(bf16[512,2048]{1,0:T(8,128)(2,1)} %all-gather.4.cloned.1.call-done) | copy-start | bytes 6291460
  110.2 2.9 copy-start.6
  118.9 1.2 copy-start.43
  118.9 1.2 copy-start.44
  119.0 1.2 copy-start.45
  119.0 1.2 copy-start.46
  119.0 1.2 copy-start.47
  119.0 1.2 copy-start.48
  119.0 1.2 copy-start.49
  119.0 1.2 copy-start.50
  119.0 1.2 copy-start.51
  119.0 1.2 copy-start.52
  119.0 1.2 copy-start.53
  119.0 1.2 copy-start.54
  119.0 1.2 copy-start.55
  119.0 1.2 copy-start.56
  119.0 1.2 copy-start.57
  119.1 1.2 copy-start.58
  119.1 4.7 %copy-start.3 = (bf16[4,64,512]{2,1,0:T(8,128)(2,1)S(1)}, bf16[4,64,512]{2,1,0:T(8,128)(2,1)}, u32[]{:S(2)}) copy-start(bf16[4,64,512]{2,1,0:T(8,128)(2,1)} %copy-done.2) | copy-start | bytes 786436
  123.5 130.7 %reduce-scatter.6.cloned.1.call-start = ((), (), s32[]{:S(2)}) async-start(), calls=%async_computation.5 | async-start | bytes 4456448 | tf_op jit(solution)/shard_map/reduce_scatter | solution.py:124
  127.7 202.6 %reduce-scatter.8.cloned.1.call-start = ((), (), s32[]{:S(2)}) async-start(), calls=%async_computation.6 | async-start | bytes 4456448 | tf_op jit(solution)/shard_map/reduce_scatter | solution.py:115
  131.3 1.3 copy-start.64
  131.3 1.4 copy-start.61
  131.3 1.5 copy-start.59
  131.3 1.5 copy-start.63
  131.3 1.5 copy-start.60
  194.5 6.6 %collective-permute-start.2 = (bf16[3,64,512]{2,1,0:T(8,128)(2,1)S(1)}, bf16[3,64,512]{2,1,0:T(8,128)(2,1)S(1)}, u32[]{:S(2)}, u32[]{:S(2)}) collective-permute-start(bf16[3,64,512]{2,1,0:T(8,128)(2,1)S(1)} %get-tuple-element.145), channel_id=1, source_target_pairs={{0,1},{1,2},{2,3},{3,4},{4,5},{5,6},{6,7},{7,8},{8,9},{9,10},{10,1... | collective-permute-start | bytes 589832 | tf_op jit(solution)/shard_map/ppermute | solution.py:15
  195.8 5.3 %collective-permute-start.3 = (bf16[3,64,512]{2,1,0:T(8,128)(2,1)S(1)}, bf16[3,64,512]{2,1,0:T(8,128)(2,1)S(1)}, u32[]{:S(2)}, u32[]{:S(2)}) collective-permute-start(bf16[3,64,512]{2,1,0:T(8,128)(2,1)S(1)} %get-tuple-element.146), channel_id=1, source_target_pairs={{1,0},{2,1},{3,2},{4,3},{5,4},{6,5},{7,6},{8,7},{9,8},{10,9},{11,1... | collective-permute-start | bytes 589832 | tf_op jit(solution)/shard_map/ppermute | solution.py:18
  200.1 1.1 copy-start.8
  200.1 1.1 copy-start.10
  200.1 1.1 copy-start.12
  200.1 1.1 copy-start.14
  200.1 1.1 copy-start.16
  (15 other events, 15.6 us)
Sparse Core Ops, SparseCore 0:
  10.1 44.2 all-gather.3
  56.6 40.1 all-gather.5
  123.6 54.3 reduce-scatter.9
  182.2 71.8 reduce-scatter.5
  258.4 71.7 reduce-scatter.7
where the time goes:
time: 337 us
  blocking collectives  133 us (39%)
  waiting for transfers between devices  126 us (37%)
  matrix products  18.4 us (5%)
  local copies, waits for them, and re-layouts  18.3 us (5%)
  other arithmetic  17.8 us (5%)
  between operations  16.9 us (5%)
  starting transfers between devices  6.71 us (2%)
    unnamed x2, blocking collectives  89.8 us
    reduce_scatter x1, waiting for transfers between devices, per_device(): lax.psum_scatter(down_full, 'row', scatter_dimension=0, tiled=True)  76.1 us
    reduce_scatter x1, waiting for transfers between devices, per_device(): lax.psum_scatter(lax.dot_general(columns, dhidden, (((0,), (0,)), ((), ()...  48.2 us
    all_gather x1, blocking collectives, per_device(): lax.all_gather(depth_weight, 'row', axis=1, tiled=True)  25.6 us
    all_gather x1, blocking collectives, per_device(): lax.all_gather(up_bias, 'row', axis=0, tiled=True)  17.5 us
    unnamed x155, local copies, waits for them, and re-layouts  7.34 us
    slice x3, local copies, waits for them, and re-layouts, depth_conv(): kernel[first * 7 + second]  6.92 us
  transfers between devices with their start and end apart: 9, of which 2 were waited for; matrix products, arithmetic and copies ran while one was open for 11% of the time, Pallas kernels for 0%

commit v1 on v0

--- a/solution.py
+++ b/solution.py
@@ -5,6 +5,27 @@
 from jax.sharding import PartitionSpec as P
 
 eps = 1e-06
+
+
+def laid_out(tiles, dim):
+    dims = list(tiles.shape[1:])
+    dims[dim] *= tiles.shape[0]
+    return jnp.moveaxis(tiles, 0, dim).reshape(dims)
+
+
+def doubled(x, axis):
+    size, index = (lax.axis_size(axis), lax.axis_index(axis))
+    tiles, bit = (x[None], 1)
+    while bit < size:
+        other = lax.ppermute(tiles, axis, [(i, i ^ bit) for i in range(size)])
+        low = index & bit == 0
+        tiles = jnp.concatenate([jnp.where(low, tiles, other), jnp.where(low, other, tiles)])
+        bit *= 2
+    return tiles
+
+
+def gather_by_bits(array, axis, dim):
+    return laid_out(doubled(array, axis), dim)
 
 
 def with_halo(block, sides, width):
@@ -71,7 +92,7 @@
     cells = height * width
     scale = 1.0 / math.sqrt(cells * devices)
     kernel, conv_bias, gain, shift, bias_down, bias_up = (
-        lax.all_gather(depth_weight, "row", axis=1, tiled=True),
+        gather_by_bits(depth_weight, "row", 1),
         lax.all_gather(depth_bias, "row", axis=0, tiled=True),
         lax.all_gather(norm_gain, "row", axis=0, tiled=True),
         lax.all_gather(norm_shift, "row", axis=0, tiled=True),

time: 337 us -> 335 us (level)
  blocking collectives: 133 us -> 111 us
  starting transfers between devices: 6.71 us -> 14.1 us
  local copies, waits for them, and re-layouts: 18.3 us -> 25.1 us
  waiting for transfers between devices: 126 us -> 130 us
    all_gather x1 -> x0, blocking collectives: 25.6 us -> none  [per_device(): lax.all_gather(depth_weight, 'row', axis=1, tiled=True)]
    ppermute x0 -> x4, starting transfers between devices: none -> 8.71 us  [doubled(): other = lax.ppermute(tiles, axis, [(i, i ^ bit) for i in range(size)])]
    ppermute x0 -> x4, waiting for transfers between devices: none -> 4.46 us  [doubled(): other = lax.ppermute(tiles, axis, [(i, i ^ bit) for i in range(size)])]
    mul x0 -> x49, local copies, waits for them, and re-layouts: none -> 3.8 us  [depth_conv(): padded[first:first + height, second:second + width, :]]
    unnamed x2, blocking collectives: 89.8 us -> 93.6 us
    unnamed x155 -> x143, local copies, waits for them, and re-layouts: 7.34 us -> 10.4 us
  transfers between devices with their start and end apart: 9 -> 13, of which waited for: 2 -> 5; matrix products, arithmetic and copies ran while one was open for 11% -> 13% of each run, Pallas kernels for 0% -> 0%
where the time goes in v1:
time: 335 us; the launch traced here: 334 us
  waiting for transfers between devices  130 us (39%)
  blocking collectives  111 us (33%)
  local copies, waits for them, and re-layouts  25.1 us (7%)
  other arithmetic  18.8 us (6%)
  matrix products  18.4 us (5%)
  between operations  16.8 us (5%)
  starting transfers between devices  14.1 us (4%)
    unnamed x2, blocking collectives  93.6 us
    reduce_scatter x1, waiting for transfers between devices, per_device(): lax.psum_scatter(down_full, 'row', scatter_dimension=0, tiled=True)  76.2 us
    reduce_scatter x1, waiting for transfers between devices, per_device(): lax.psum_scatter(lax.dot_general(columns, dhidden, (((0,), (0,)), ((), ()...  48.3 us
    all_gather x1, blocking collectives, per_device(): lax.all_gather(up_bias, 'row', axis=0, tiled=True)  17.3 us
    unnamed x143, local copies, waits for them, and re-layouts  10.4 us
    ppermute x4, starting transfers between devices, doubled(): other = lax.ppermute(tiles, axis, [(i, i ^ bit) for i in range(size)])  8.71 us
    slice x3, local copies, waits for them, and re-layouts, depth_conv(): kernel[first * 7 + second]  6.84 us
  transfers between devices with their start and end apart: 13, of which 5 were waited for; matrix products, arithmetic and copies ran while one was open for 13% of the time, Pallas kernels for 0%

profile of v1, /device:TPU:0, one launch (start us, length us, event | category | flops | bytes accessed | tf_op | source)
XLA Modules:
  0.0 333.9 jit_solution(106703681211687526)
XLA Ops:
  7.2 0.7 all-gather.4.cloned.1.call-update
  8.0 0.6 collective-permute-start.2
  8.5 0.1 all-gather.6.cloned.1.call-update
  8.7 0.8 collective-permute-done.2
  9.6 0.7 broadcast_select_fusion.7
  10.3 2.9 collective-permute-start.3
  13.2 1.7 collective-permute-done.3
  14.9 2.1 collective-permute-start.4
  17.1 1.9 collective-permute-done.4
  19.0 3.1 collective-permute-start.5
  22.1 1.0 fusion.148
  23.2 1.3 collective-permute-start
  24.5 1.3 collective-permute-start.1
  25.8 1.3 fusion.149
  27.8 0.9 dynamic-update-slice
  28.6 0.8 dynamic-update-slice.1
  29.5 0.8 dynamic-update-slice.2
  30.3 0.8 dynamic-update-slice.3
  31.2 34.2 %all-reduce.12 = (bf16[512]{0:T(512)(128)(2,1)S(1)}, bf16[512]{0:T(512)(128)(2,1)S(1)}, bf16[512]{0:T(512)(128)(2,1)S(1)}, bf16[512]{0:T(512)(128)(2,1)}) all-reduce(bf16[512]{0:T(512)(128)(2,1)S(1)} %dynamic-update-slice, bf16[512]{0:T(512)(128)(2,1)S(1)} %dynamic-update-slice.2, ...), channel_id=1, replica_groups=mesh['groups'=2,'row'=16] {'row'}, use_global_device_ids=true, to_apply=%add.2 | all-reduce | flops 2048 | bytes 8192
  65.4 17.3 %all-gather = bf16[16,1,128]{2,1,0:T(2,128)(2,1)S(1)} all-gather(bf16[1,1,128]{2,1,0:T(2,128)(2,1)} %bitcast.137), channel_id=1, replica_groups=mesh['groups'=2,'row'=16] {'row'}, dimensions={0}, use_global_device_ids=true | all-gather | bytes 4352 | tf_op jit(solution)/shard_map/all_gather | solution.py:100
  82.8 2.6 slice_reduce_fusion.48
  85.4 2.7 slice_reduce_fusion.47
  88.1 0.1 mul.1051
  90.6 0.1 mul.1180
  90.7 0.1 mul.1183
  90.8 0.1 mul.1186
  90.8 0.1 mul.1189
  90.9 0.1 mul.1192
  91.0 0.1 mul.1195
  91.1 1.6 slice_reduce_fusion.46
  92.7 0.1 mul.1057
  93.6 0.1 maximum_convert_fusion
  93.8 4.9 %fusion.146 = (f32[4,64]{1,0:T(4,128)S(1)}, f32[4,64,512]{2,1,0:T(8,128)S(1)}) fusion(f32[512]{0:T(512)S(1)} %convert_element_type.67, f32[512]{0:T(512)S(1)} %mul.1195, f32[512]{0:T(512)S(1)} %mul.1192, f32[512]{0:T(512)S(1)} %mul.1189, f32[512]{0:T(512)S(1)} %mul.1186, f32[10,64,512]{2,1,0:T(8,128)S(1)} %maximum_convert_fusion, f32[512]{0:T(512)S(1)} %mul.1183, ...), kind=kLoop, calls=%fused_computation.380 | loop fusion | flops 12975872 | bytes 5608448 | tf_op jit(solution)/shard_map/reduce_sum | solution.py:107
  98.8 0.2 multiply_reduce_fusion.3
  99.0 0.2 add_convert_fusion.1
  99.2 3.8 %multiply_convert_fusion = (bf16[256,2048]{1,0:T(8,128)(2,1)S(1)}, f32[256,2048]{1,0:T(8,128)}) fusion(f32[2048]{0:T(1024)S(1)} %bitcast.86, bf16[256,512]{1,0:T(8,128)(2,1)S(1)} %bitcast.80, bf16[512,2048]{1,0:T(8,128)(2,1)} %all-gather.4.cloned.1.call-done), kind=kOutput, calls=%fused_computation.61 | convolution fusion | flops 540016640 | bytes 5513216 | tf_op jit(solution)/shard_map/dot_general | solution.py:116
  103.0 4.2 %convert_reduce_fusion.1 = (f32[2048]{0:T(1024)}, bf16[256,2048]{1,0:T(8,128)(2,1)S(1)}) fusion(f32[256,2048]{1,0:T(8,128)} %get-tuple-element.160, bf16[256,512]{1,0:T(8,128)(2,1)} %bitcast.82, bf16[2048,512]{1,0:T(8,128)(2,1)} %all-gather.6.cloned.1.call-done), kind=kOutput, calls=%fused_computation.60 | convolution fusion | flops 543160320 | bytes 5513216 | tf_op jit(solution)/shard_map/dot_general | solution.py:137
  107.3 1.3 fusion.145
  108.6 0.8 copy-done
  109.4 0.8 multiply_reduce_fusion
  110.2 0.6 broadcast_multiply_fusion.6
  110.8 0.7 div.17
  111.5 3.2 fusion.143
  114.6 1.4 fusion.142
  116.1 1.0 fusion.144
  117.4 2.3 stack.199
  119.7 0.9 copy.22
  120.6 3.9 %convolution_multiply_fusion.1 = f32[512,2048]{1,0:T(8,128)} fusion(bf16[256,512]{1,0:T(8,128)(2,1)S(1)} %bitcast.81, bf16[256,2048]{1,0:T(8,128)(2,1)} %copy-done.6), kind=kOutput, calls=%fused_computation.51 | convolution fusion | flops 537919488 | bytes 5505024 | tf_op jit(solution)/shard_map/dot_general | solution.py:146
  124.6 0.9 copy-done.4
  125.4 2.7 convolution_multiply_fusion
  129.7 59.4 %all-reduce.11 = (f32[512]{0:T(512)S(1)}, f32[512]{0:T(512)S(1)}, f32[512]{0:T(512)S(1)}, f32[2048]{0:T(1024)S(1)}, f32[512]{0:T(512)S(1)}) all-reduce(f32[512]{0:T(512)S(1)} %broadcast_multiply_fusion.5, f32[512]{0:T(512)S(1)} %get-tuple-element.165, ...), channel_id=5, replica_groups=mesh['groups'=2,'row'=16] {'row'}, use_global_device_ids=true, to_apply=%region_57.58.clone | all-reduce | flops 4096 | bytes 32768
  189.0 0.6 dynamic-slice.13
  189.6 0.6 dynamic-slice.9
  190.2 0.6 dynamic-slice.7
  190.8 0.6 dynamic-slice.5
  191.4 1.3 collective-permute-start.6
  192.7 1.3 collective-permute-start.7
  194.0 0.6 dynamic-slice.11
  194.6 2.4 convolution_add_fusion.1
  197.2 0.8 add_convert_fusion
  198.0 0.1 maximum_convert_fusion.1
  198.2 4.7 %fusion.5 = bf16[4,64,512]{2,1,0:T(8,128)(2,1)} fusion(bf16[4,64,512]{2,1,0:T(8,128)(2,1)S(1)} %copy-done.4, f32[10,64,512]{2,1,0:T(8,128)S(1)} %maximum_convert_fusion.1, f32[512]{0:T(512)S(1)} %copy-done.20, f32[512]{0:T(512)S(1)} %copy-done.18, f32[512]{0:T(512)S(1)} %copy-done.16, f32[512]{0:T(512)S(1)} %copy-done.14, f32[512]{0:T(512)S(1)} %copy-done.12, ...), kind=kLoop, calls=%fused_computation.152 | loop fusion | flops 13107200 | bytes 5605376 | tf_op jit(solution)/shard_map/convert_element_type | solution.py:183
  202.9 48.3 %reduce-scatter.6.cloned.1.call-done = f32[32,2048]{1,0:T(8,128)} async-done(((f32[512,2048]{1,0:T(8,128)}), f32[32,2048]{1,0:T(8,128)}) %reduce-scatter.6.cloned.1.call-update) | async-done | bytes 262160 | tf_op jit(solution)/shard_map/reduce_scatter | solution.py:145
  251.2 76.2 %reduce-scatter.8.cloned.1.call-done = f32[128,512]{1,0:T(8,128)} async-done(((f32[2048,512]{1,0:T(8,128)}), f32[128,512]{1,0:T(8,128)}) %reduce-scatter.8.cloned.1.call-update) | async-done | bytes 262160 | tf_op jit(solution)/shard_map/reduce_scatter | solution.py:136
  (209 shorter events, 4.0 us)
Async XLA Ops:
  7.2 92.0 %all-gather.4.cloned.1.call-start = ((), (), s32[]{:S(2)}) async-start(), calls=%async_computation.3 | async-start | bytes 2228224 | tf_op jit(solution)/shard_map/all_gather | solution.py:118
  7.9 95.1 %all-gather.6.cloned.1.call-start = ((), (), s32[]{:S(2)}) async-start(), calls=%async_computation.4 | async-start | bytes 2228224 | tf_op jit(solution)/shard_map/all_gather | solution.py:125
  8.0 1.6 collective-permute-start.2
  8.7 194.2 %reduce-scatter.10.cloned.1.call-start = ((), (), s32[]{:S(2)}) async-start(), calls=%async_computation.7 | async-start | bytes 278528
  10.3 4.6 %collective-permute-start.3 = (bf16[2,49,32]{1,2,0:T(8,128)(2,1)S(1)}, bf16[2,49,32]{1,2,0:T(8,128)(2,1)S(1)}, u32[]{:S(2)}, u32[]{:S(2)}) collective-permute-start(bf16[2,49,32]{1,2,0:T(8,128)(2,1)S(1)} %pad_maximum_fusion.2), channel_id=1, source_target_pairs={{0,2},{1,3},{2,0},{3,1},{4,6},{5,7},{6,4},{7,5},{8,10},{9,11},{10,... | collective-permute-start | bytes 18824 | tf_op jit(solution)/shard_map/ppermute | solution.py:20
  14.9 4.0 %collective-permute-start.4 = (bf16[4,49,32]{1,2,0:T(8,128)(2,1)S(1)}, bf16[4,49,32]{1,2,0:T(8,128)(2,1)S(1)}, u32[]{:S(2)}, u32[]{:S(2)}) collective-permute-start(bf16[4,49,32]{1,2,0:T(8,128)(2,1)S(1)} %pad_maximum_fusion.1), channel_id=1, source_target_pairs={{0,4},{1,5},{2,6},{3,7},{4,0},{5,1},{6,2},{7,3},{8,12},{9,13},{10,... | collective-permute-start | bytes 37640 | tf_op jit(solution)/shard_map/ppermute | solution.py:20
  19.0 63.7 %collective-permute-start.5 = (bf16[8,49,32]{1,2,0:T(8,128)(2,1)S(1)}, bf16[8,49,32]{1,2,0:T(8,128)(2,1)S(1)}, u32[]{:S(2)}, u32[]{:S(2)}) collective-permute-start(bf16[8,49,32]{1,2,0:T(8,128)(2,1)S(1)} %pad_maximum_fusion), channel_id=1, source_target_pairs={{0,8},{1,9},{2,10},{3,11},{4,12},{5,13},{6,14},{7,15},{8,0},{9,1},... | collective-permute-start | bytes 75272 | tf_op jit(solution)/shard_map/ppermute | solution.py:20
  23.2 70.4 %collective-permute-start = (bf16[3,64,512]{2,1,0:T(8,128)(2,1)S(1)}, bf16[3,64,512]{2,1,0:T(8,128)(2,1)S(1)}, u32[]{:S(2)}, u32[]{:S(2)}) collective-permute-start(bf16[3,64,512]{2,1,0:T(8,128)(2,1)S(1)} %get-tuple-element.147), channel_id=1, source_target_pairs={{0,1},{1,2},{2,3},{3,4},{4,5},{5,6},{6,7},{7,8},{8,9},{9,10},{10,1... | collective-permute-start | bytes 589832 | tf_op jit(solution)/shard_map/ppermute | solution.py:36
  24.5 69.1 %collective-permute-start.1 = (bf16[3,64,512]{2,1,0:T(8,128)(2,1)S(1)}, bf16[3,64,512]{2,1,0:T(8,128)(2,1)S(1)}, u32[]{:S(2)}, u32[]{:S(2)}) collective-permute-start(bf16[3,64,512]{2,1,0:T(8,128)(2,1)S(1)} %get-tuple-element.148), channel_id=1, source_target_pairs={{1,0},{2,1},{3,2},{4,3},{5,4},{6,5},{7,6},{8,7},{9,8},{10,9},{11,1... | collective-permute-start | bytes 589832 | tf_op jit(solution)/shard_map/ppermute | solution.py:39
  88.1 5.5 %copy-start.1 = (bf16[4,64,512]{2,1,0:T(8,128)(2,1)S(1)}, bf16[4,64,512]{2,1,0:T(8,128)(2,1)}, u32[]{:S(2)}) copy-start(bf16[4,64,512]{2,1,0:T(8,128)(2,1)} %param.10) | copy-start | bytes 786436
  90.6 3.1 copy-start.7
  90.7 3.0 copy-start.9
  90.8 3.0 copy-start.11
  90.8 2.9 copy-start.13
  90.9 2.8 copy-start.15
  91.0 2.7 copy-start.17
  91.1 2.7 copy-start.19
  92.8 5.9 %copy-start.21 = (f32[512]{0:T(512)}, f32[512]{0:T(512)S(1)}, u32[]{:S(2)}) copy-start(f32[512]{0:T(512)S(1)} %mul.1057) | copy-start | bytes 6148
  92.8 5.8 %copy-start.23 = (f32[512]{0:T(512)}, f32[512]{0:T(512)S(1)}, u32[]{:S(2)}) copy-start(f32[512]{0:T(512)S(1)} %mul.1060) | copy-start | bytes 6148
  92.9 5.8 %copy-start.25 = (f32[512]{0:T(512)}, f32[512]{0:T(512)S(1)}, u32[]{:S(2)}) copy-start(f32[512]{0:T(512)S(1)} %mul.1063) | copy-start | bytes 6148
  93.0 5.7 %copy-start.27 = (f32[512]{0:T(512)}, f32[512]{0:T(512)S(1)}, u32[]{:S(2)}) copy-start(f32[512]{0:T(512)S(1)} %mul.1066) | copy-start | bytes 6148
  93.1 5.6 %copy-start.29 = (f32[512]{0:T(512)}, f32[512]{0:T(512)S(1)}, u32[]{:S(2)}) copy-start(f32[512]{0:T(512)S(1)} %mul.1069) | copy-start | bytes 6148
  93.2 5.5 %copy-start.31 = (f32[512]{0:T(512)}, f32[512]{0:T(512)S(1)}, u32[]{:S(2)}) copy-start(f32[512]{0:T(512)S(1)} %mul.1072) | copy-start | bytes 6148
  93.2 5.5 %copy-start.33 = (f32[512]{0:T(512)}, f32[512]{0:T(512)S(1)}, u32[]{:S(2)}) copy-start(f32[512]{0:T(512)S(1)} %mul.1075) | copy-start | bytes 6148
  93.3 5.4 %copy-start.35 = (f32[512]{0:T(512)}, f32[512]{0:T(512)S(1)}, u32[]{:S(2)}) copy-start(f32[512]{0:T(512)S(1)} %mul.1078) | copy-start | bytes 6148
  93.4 5.3 %copy-start.37 = (f32[512]{0:T(512)}, f32[512]{0:T(512)S(1)}, u32[]{:S(2)}) copy-start(f32[512]{0:T(512)S(1)} %mul.1081) | copy-start | bytes 6148
  93.5 5.3 %copy-start.39 = (f32[512]{0:T(512)}, f32[512]{0:T(512)S(1)}, u32[]{:S(2)}) copy-start(f32[512]{0:T(512)S(1)} %mul.1084) | copy-start | bytes 6148
  93.6 5.2 %copy-start.41 = (f32[512]{0:T(512)}, f32[512]{0:T(512)S(1)}, u32[]{:S(2)}) copy-start(f32[512]{0:T(512)S(1)} %mul.1087) | copy-start | bytes 6148
  99.2 3.9 %copy-start.2 = (bf16[4,64,512]{2,1,0:T(8,128)(2,1)}, bf16[4,64,512]{2,1,0:T(8,128)(2,1)S(1)}, u32[]{:S(2)}) copy-start(bf16[4,64,512]{2,1,0:T(8,128)(2,1)S(1)} %add_convert_fusion.1) | copy-start | bytes 786436
  103.0 4.2 %copy-start.5 = (bf16[512,2048]{1,0:T(8,128)(2,1)S(1)}, bf16[512,2048]{1,0:T(8,128)(2,1)}, u32[]{:S(2)}) copy-start(bf16[512,2048]{1,0:T(8,128)(2,1)} %all-gather.4.cloned.1.call-done) | copy-start | bytes 6291460
  107.3 2.9 copy-start.6
  116.0 1.2 copy-start.43
  116.0 1.2 copy-start.44
  116.0 1.2 copy-start.45
  116.0 1.2 copy-start.46
  116.0 1.2 copy-start.47
  116.0 1.2 copy-start.48
  116.0 1.2 copy-start.49
  116.0 1.2 copy-start.50
  116.1 1.2 copy-start.51
  116.1 1.2 copy-start.52
  116.1 1.2 copy-start.53
  116.1 1.2 copy-start.54
  116.1 1.2 copy-start.55
  116.1 1.2 copy-start.56
  116.1 1.2 copy-start.57
  116.1 1.2 copy-start.58
  116.1 4.5 %copy-start.3 = (bf16[4,64,512]{2,1,0:T(8,128)(2,1)S(1)}, bf16[4,64,512]{2,1,0:T(8,128)(2,1)}, u32[]{:S(2)}) copy-start(bf16[4,64,512]{2,1,0:T(8,128)(2,1)} %copy-done.2) | copy-start | bytes 786436
  120.5 130.7 %reduce-scatter.6.cloned.1.call-start = ((), (), s32[]{:S(2)}) async-start(), calls=%async_computation.5 | async-start | bytes 4456448 | tf_op jit(solution)/shard_map/reduce_scatter | solution.py:145
  124.5 202.8 %reduce-scatter.8.cloned.1.call-start = ((), (), s32[]{:S(2)}) async-start(), calls=%async_computation.6 | async-start | bytes 4456448 | tf_op jit(solution)/shard_map/reduce_scatter | solution.py:136
  128.2 1.3 copy-start.63
  128.2 1.4 copy-start.61
  128.2 1.5 copy-start.59
  128.2 1.5 copy-start.62
  128.2 1.5 copy-start.60
  191.4 6.6 %collective-permute-start.6 = (bf16[3,64,512]{2,1,0:T(8,128)(2,1)S(1)}, bf16[3,64,512]{2,1,0:T(8,128)(2,1)S(1)}, u32[]{:S(2)}, u32[]{:S(2)}) collective-permute-start(bf16[3,64,512]{2,1,0:T(8,128)(2,1)S(1)} %get-tuple-element.145), channel_id=1, source_target_pairs={{0,1},{1,2},{2,3},{3,4},{4,5},{5,6},{6,7},{7,8},{8,9},{9,10},{10,1... | collective-permute-start | bytes 589832 | tf_op jit(solution)/shard_map/ppermute | solution.py:36
  192.7 5.2 %collective-permute-start.7 = (bf16[3,64,512]{2,1,0:T(8,128)(2,1)S(1)}, bf16[3,64,512]{2,1,0:T(8,128)(2,1)S(1)}, u32[]{:S(2)}, u32[]{:S(2)}) collective-permute-start(bf16[3,64,512]{2,1,0:T(8,128)(2,1)S(1)} %get-tuple-element.146), channel_id=1, source_target_pairs={{1,0},{2,1},{3,2},{4,3},{5,4},{6,5},{7,6},{8,7},{9,8},{10,9},{11,1... | collective-permute-start | bytes 589832 | tf_op jit(solution)/shard_map/ppermute | solution.py:39
  197.0 1.1 copy-start.8
  197.0 1.1 copy-start.10
  197.0 1.1 copy-start.12
  197.0 1.1 copy-start.14
  197.0 1.1 copy-start.16
  197.1 1.1 copy-start.18
  197.1 1.1 copy-start.20
  (13 other events, 13.5 us)
Sparse Core Ops, SparseCore 0:
  10.1 45.4 all-gather.3
  57.8 40.3 all-gather.5
  120.7 54.3 reduce-scatter.9
  179.3 71.8 reduce-scatter.5
  255.5 71.8 reduce-scatter.7
